TPU v7x, 256 devices: a whole 4x4x8 slice. The times are simulated.
256 devices in a mesh: stream: 2 (over z_hi), dp: 16 (over x, y), tensor: 8 (over z_lo, core).
Axes of the slice: x: 4, y: 4, z: 8 (z_hi: 2, z_lo: 4; z = z_hi * 4 + z_lo), core: 2. Of those that a mesh axis runs over, the one named last changes fastest.
Arguments:
- hidden: bfloat16 [2, 256, 8192], P('stream', 'tensor', 'dp'), may hold values from -3 to 3
- cached_rotated_keys: bfloat16 [2, 256, 8, 256, 128], P('stream', 'dp', 'tensor'), may hold values from -6 to 6
- cached_values: bfloat16 [2, 256, 8, 256, 128], P('stream', 'dp', 'tensor'), may hold values from -18 to 18
- cache_lengths: int32 [2, 256], P('stream', 'dp'), may hold values from 1 to 256, as said below
- recent_ids: int32 [256, 128], replicated, may hold values from 0 to 65535
- guidance: float32 [256], replicated, may hold values from 1 to 3
- w_query: bfloat16 [8192, 8192], P('dp', 'tensor'), may hold values from -0.0625 to 0.0625
- key_value_weight: bfloat16 [8192, 2, 1024], P('dp', None, 'tensor'), may hold values from -0.0625 to 0.0625
- w_output: bfloat16 [8192, 8192], P('tensor', 'dp'), may hold values from -0.0625 to 0.0625
- norm_gain: bfloat16 [8192], P('dp'), may hold values from 0.5 to 1.5
- w_head: bfloat16 [8192, 65536], P(None, ('dp', 'tensor')), may hold values from -0.16503906 to 0.16503906
Outputs:
- guided_logprobs: float32 [256, 65536], P('stream', ('dp', 'tensor'))
Inputs may be any that keep to these rules, and one draw needn't show every extreme that they name: `cache_lengths`: every prompt has 1 to 256 filled slots in each stream; some prompt has all 256; lengths differ widely from one group of 16 prompts to the next.
All inputs are finite; a program needn't handle non-finite values.
Results may differ from a plain program's by a relative error of at most 0.0025.
Values may be sent and summed in bfloat16 or wider, within the bound.
A program may use at most 64 MiB of HBM per device.

v0:
```python
import jax
import jax.numpy as jnp
from jax import lax
from jax.sharding import PartitionSpec as P

MODEL_WIDTH = 8192
HEAD_SIZE = 128
rope_theta = 500000.0
penalty_step = 1.5
norm_eps = 1e-05


def partner_2(value, axis, distance):
    mask = 2**distance
    pairs = [(source, source ^ mask) for source in range(lax.axis_size(axis))]
    return lax.ppermute(value, axis, pairs)


def rotate(values, positions):
    halfway = values.shape[-1] // 2
    frequency = rope_theta ** (-(jnp.arange(halfway, dtype=jnp.float32) * 2.0 / values.shape[-1]))
    angles = positions.astype(jnp.float32)[:, None, None] * frequency
    cosine_term = jnp.cos(angles)
    sine_term = jnp.sin(angles)
    first_half = values[..., :halfway]
    second_half = values[..., halfway:]
    return jnp.concatenate(
        [
            first_half * cosine_term - second_half * sine_term,
            second_half * cosine_term + first_half * sine_term,
        ],
        axis=-1,
    )


def repeat_counts(recent_ids, first_column, width):
    columns = first_column + jnp.arange(width, dtype=jnp.int32)
    return jnp.sum((recent_ids[:, :, None] == columns[None, None, :]).astype(jnp.float32), 1)


def body(
    hidden,
    cached_rotated_keys,
    cached_values,
    cache_lengths,
    recent_ids,
    guidance,
    w_query,
    key_value_weight,
    w_output,
    norm_gain,
    w_head,
):
    local_width = hidden.shape[2]
    query_cols = w_query.shape[1]
    kv_cols = key_value_weight.shape[2]
    local_prompts = cache_lengths.shape[1]
    lengths = cache_lengths[0]
    vocab_local = w_head.shape[1]
    all_rows = lax.all_gather(hidden[0], "tensor", axis=0, tiled=True)
    kv_flat = key_value_weight.reshape(local_width, 2 * kv_cols)
    projected = lax.psum_scatter(
        jnp.concatenate(
            [
                jnp.dot(all_rows, w_query, preferred_element_type=jnp.float32),
                jnp.dot(all_rows, kv_flat, preferred_element_type=jnp.float32),
            ],
            axis=1,
        ),
        "dp",
        scatter_dimension=0,
        tiled=True,
    )
    query_heads = query_cols // HEAD_SIZE
    kv_heads = kv_cols // HEAD_SIZE
    rotated_query = rotate(
        projected[:, :query_cols].reshape(local_prompts, query_heads, HEAD_SIZE), lengths
    ).astype(jnp.bfloat16)
    key_value_rows = projected[:, query_cols:].reshape(local_prompts, 2, kv_heads, HEAD_SIZE)
    fresh_key = rotate(key_value_rows[:, 0], lengths).astype(jnp.bfloat16)
    value_new = key_value_rows[:, 1].astype(jnp.bfloat16)
    grouped_queries = rotated_query.reshape(
        local_prompts, kv_heads, query_heads // kv_heads, HEAD_SIZE
    )
    attention_scale = HEAD_SIZE ** (-0.5)
    key_block = cached_rotated_keys[0]
    value_block = cached_values[0]
    scores = (
        jnp.einsum(
            "pkgd,pksd->pkgs", grouped_queries, key_block, preferred_element_type=jnp.float32
        )
        * attention_scale
    )
    self_score = (
        jnp.einsum("pkgd,pkd->pkg", grouped_queries, fresh_key, preferred_element_type=jnp.float32)
        * attention_scale
    )
    valid = jnp.arange(key_block.shape[2], dtype=jnp.int32)[None, :] < lengths[:, None]
    exps = jnp.where(valid[:, None, None, :], jnp.exp(scores), 0.0)
    own_exp = jnp.exp(self_score)
    denominator = jnp.sum(exps, -1) + own_exp
    weights = (exps / denominator[..., None]).astype(jnp.bfloat16)
    own_weight = (own_exp / denominator).astype(jnp.bfloat16)
    attended = jnp.einsum(
        "pkgs,pksd->pkgd", weights, value_block, preferred_element_type=jnp.float32
    )
    attended = (
        attended
        + own_weight.astype(jnp.float32)[..., None] * value_new.astype(jnp.float32)[:, :, None, :]
    )
    attended = attended.reshape(local_prompts, query_cols).astype(jnp.bfloat16)
    partial_out = jnp.dot(
        lax.all_gather(attended, "dp", axis=0, tiled=True),
        w_output,
        preferred_element_type=jnp.float32,
    )
    output_sum = lax.psum_scatter(partial_out, "tensor", scatter_dimension=0, tiled=True)
    residual = (hidden[0].astype(jnp.float32) + output_sum).astype(jnp.bfloat16)
    widened = residual.astype(jnp.float32)
    squares = lax.psum(jnp.sum(widened * widened, 1), "dp")
    inverse = lax.rsqrt(squares / MODEL_WIDTH + norm_eps)
    normed = (widened * inverse[:, None] * norm_gain.astype(jnp.float32)).astype(jnp.bfloat16)
    normed_all = lax.all_gather(normed, "tensor", axis=0, tiled=True)
    logits = jnp.dot(
        lax.all_gather(normed_all, "dp", axis=1, tiled=True),
        w_head,
        preferred_element_type=jnp.float32,
    )
    stream_side = lax.axis_index("stream")
    half_rows = logits.shape[0] // 2
    mine_start = stream_side * half_rows
    other_start = (1 - stream_side) * half_rows
    column_base = lax.axis_index(("dp", "tensor")) * vocab_local
    mine = lax.dynamic_slice_in_dim(logits, mine_start, half_rows, 0)
    sending = lax.dynamic_slice_in_dim(logits, other_start, half_rows, 0)
    partner = partner_2(sending, "stream", 0)
    conditional = jnp.where(stream_side == 0, mine, partner)
    unconditional = jnp.where(stream_side == 0, partner, mine)
    guide = lax.dynamic_slice_in_dim(guidance, mine_start, half_rows, 0)[:, None]
    recent_mine = lax.dynamic_slice_in_dim(recent_ids, mine_start, half_rows, 0)
    guided = unconditional + guide * (conditional - unconditional)
    guided = guided - penalty_step * repeat_counts(recent_mine, column_base, vocab_local)
    totals = lax.psum(jnp.sum(jnp.exp(guided), 1), ("dp", "tensor"))
    return guided - jnp.log(totals)[:, None]


def solution(mesh):
    return jax.shard_map(
        body,
        mesh=mesh,
        in_specs=(
            P("stream", "tensor", "dp"),
            P("stream", "dp", "tensor", None, None),
            P("stream", "dp", "tensor", None, None),
            P("stream", "dp"),
            P(),
            P(),
            P("dp", "tensor"),
            P("dp", None, "tensor"),
            P("tensor", "dp"),
            P("dp"),
            P(None, ("dp", "tensor")),
        ),
        out_specs=P("stream", ("dp", "tensor")),
        check_vma=False,
    )
```

profile of v0, /device:TPU:128, one launch (start us, length us, event | category | flops | bytes accessed | tf_op | source)
XLA Modules:
  0.0 647.4 jit_solution(1154850240006349418)
XLA Ops:
  6.5 0.0 copy-start
  6.5 0.0 copy-start.6
  6.6 0.0 copy-start.4
  6.6 0.0 reduce-scatter.3.cloned.1.call-start
  6.6 14.5 %all-gather = bf16[1,256,512]{2,1,0:T(8,128)(2,1)S(1)} all-gather(bf16[1,32,512]{2,1,0:T(8,128)(2,1)} %param.11), channel_id=2, replica_groups=mesh['stream'=2,'dp'=16,'tensor'=8] {'tensor'}, dimensions={1}, use_global_device_ids=true | all-gather | bytes 294912 | tf_op jit(solution)/shard_map/all_gather | solution.py:60
  21.1 0.0 copy-done
  21.1 0.5 fusion.9
  21.6 1.2 fusion.5
  22.8 1.2 pad_maximum_fusion
  24.0 0.0 reduce-scatter.3.cloned.1.call-update
  24.0 0.0 reduce-scatter.5.cloned.1.call-start
  24.1 0.7 bitcast_convert_fusion
  24.7 0.7 iota_compare_fusion
  25.4 0.1 multiply_cosine_fusion.1
  25.6 79.2 %reduce-scatter.3.cloned.1.call-done = f32[16,1280]{1,0:T(8,128)} async-done(((f32[256,1280]{1,0:T(8,128)}), f32[16,1280]{1,0:T(8,128)}) %reduce-scatter.3.cloned.1.call-update) | async-done | bytes 81936 | tf_op jit(solution)/shard_map/reduce_scatter | solution.py:62
  104.8 0.7 slice.36
  105.6 0.1 fusion.30
  105.7 0.8 slice_bitcast_fusion
  106.6 0.1 maximum_bitcast_fusion
  106.6 0.1 subtract_convert_fusion
  106.7 0.2 fusion.25
  106.9 1.7 fusion.33
  108.7 0.0 copy-done.1
  108.7 0.3 fusion.2
  109.0 23.3 %all_gather.13 = bf16[256,1024]{1,0:T(8,128)(2,1)S(1)} all-gather(bf16[16,1024]{1,0:T(8,128)(2,1)S(1)} %bitcast.51), channel_id=1, replica_groups=mesh['stream'=2,'dp'=16,'tensor'=8] {'dp'}, dimensions={0}, use_global_device_ids=true | all-gather | bytes 557056 | tf_op jit(solution)/shard_map/all_gather | solution.py:113
  132.3 0.0 copy-done.2
  132.3 1.2 fusion.34
  133.5 0.0 reduce-scatter.5.cloned.1.call-update
  133.6 0.0 all-gather.3.cloned.1.call-start
  133.6 0.0 copy-done.5
  133.6 32.9 %reduce-scatter.5.cloned.1.call-done = f32[32,512]{1,0:T(8,128)} async-done(((f32[256,512]{1,0:T(8,128)}), f32[32,512]{1,0:T(8,128)}) %reduce-scatter.5.cloned.1.call-update) | async-done | bytes 65552 | tf_op jit(solution)/shard_map/reduce_scatter | solution.py:117
  166.5 0.0 copy-done.3
  166.5 1.0 fusion.11
  167.5 40.3 %psum.14 = f32[32]{0:T(128)S(1)} all-reduce(f32[32]{0:T(128)S(1)} %fusion.11), channel_id=1, replica_groups=mesh['stream'=2,'dp'=16,'tensor'=8] {'dp'}, use_global_device_ids=true, to_apply=%region_4.5 | all-reduce | flops 32 | bytes 256 | tf_op jit(solution)/shard_map/psum | solution.py:120
  207.8 0.9 fusion.13
  208.7 15.3 %all_gather.14 = bf16[256,512]{1,0:T(8,128)(2,1)} all-gather(bf16[32,512]{1,0:T(8,128)(2,1)S(1)} %fusion.13), channel_id=1, replica_groups=mesh['stream'=2,'dp'=16,'tensor'=8] {'tensor'}, dimensions={0}, use_global_device_ids=true | all-gather | bytes 294912 | tf_op jit(solution)/shard_map/all_gather | solution.py:123
  224.0 0.0 all-gather.3.cloned.1.call-update
  224.1 0.0 copy-done.6
  224.1 0.1 dynamic_slice.14
  224.2 0.0 copy-done.4
  224.2 58.3 %all-gather.3.cloned.1.call-done = bf16[256,8192]{1,0:T(8,128)(2,1)} async-done(((bf16[256,512]{1,0:T(8,128)(2,1)}), bf16[256,8192]{1,0:T(8,128)(2,1)}) %all-gather.3.cloned.1.call-update) | async-done | bytes 4194320 | tf_op jit(solution)/shard_map/all_gather | solution.py:125
  282.5 7.0 %fusion.35 = f32[256,512]{1,0:T(8,128)S(1)} fusion(bf16[256,8192]{1,0:T(8,128)(2,1)} %all-gather.3.cloned.1.call-done, bf16[8192,512]{1,0:T(8,128)(2,1)} %param.21), kind=kOutput, calls=%fused_computation.66 | convolution fusion | flops 2147483648 | bytes 13107200 | tf_op jit(solution)/shard_map/dot_general | solution.py:124
  289.5 0.3 collective-permute-start
  289.8 4.7 convert_reduce_fusion
  294.4 11.4 %collective-permute-done = f32[128,512]{1,0:T(8,128)S(1)} collective-permute-done((f32[128,512]{1,0:T(8,128)S(1)}, f32[128,512]{1,0:T(8,128)S(1)}, u32[]{:S(2)}, u32[]{:S(2)}) %collective-permute-start) | collective-permute-done | bytes 262176 | tf_op jit(solution)/shard_map/ppermute | solution.py:16
  305.8 0.2 exponential_reduce_fusion
  306.0 334.1 %psum.15 = f32[128]{0:T(128)S(1)} all-reduce(f32[128]{0:T(128)S(1)} %get-tuple-element.5), channel_id=1, replica_groups=mesh['stream'=2,'dp'=16,'tensor'=8] {'dp','tensor'}, use_global_device_ids=true, to_apply=%region_7.8 | all-reduce | flops 128 | bytes 1024 | tf_op jit(solution)/shard_map/psum | solution.py:143
  640.1 0.8 broadcast_subtract_fusion
  (17 shorter events, 0.2 us)
Async XLA Ops:
  6.5 14.6 %copy-start = (bf16[512,1024]{1,0:T(8,128)(2,1)S(1)}, bf16[512,1024]{1,0:T(8,128)(2,1)}, u32[]{:S(2)}) copy-start(bf16[512,1024]{1,0:T(8,128)(2,1)} %param.17) | copy-start | bytes 3145732
  6.5 160.0 %copy-start.3 = (bf16[1,32,512]{2,1,0:T(8,128)(2,1)S(1)}, bf16[1,32,512]{2,1,0:T(8,128)(2,1)}, u32[]{:S(2)}) copy-start(bf16[1,32,512]{2,1,0:T(8,128)(2,1)} %param.11) | copy-start | bytes 98308
  6.5 102.2 %copy-start.1 = (bf16[1,16,1,256,128]{4,3,2,1,0:T(8,128)(2,1)S(1)}, bf16[1,16,1,256,128]{4,3,2,1,0:T(8,128)(2,1)}, u32[]{:S(2)}) copy-start(bf16[1,16,1,256,128]{4,3,2,1,0:T(8,128)(2,1)} %param.13) | copy-start | bytes 3145732
  6.5 125.8 %copy-start.2 = (bf16[1024,512]{1,0:T(8,128)(2,1)S(1)}, bf16[1024,512]{1,0:T(8,128)(2,1)}, u32[]{:S(2)}) copy-start(bf16[1024,512]{1,0:T(8,128)(2,1)} %param.19) | copy-start | bytes 3145732
  6.5 127.1 %copy-start.5 = (bf16[512]{0:T(512)(128)(2,1)S(1)}, bf16[512]{0:T(512)(128)(2,1)}, u32[]{:S(2)}) copy-start(bf16[512]{0:T(512)(128)(2,1)} %param.20) | copy-start | bytes 3076
  6.5 217.5 %copy-start.6 = (f32[256]{0:T(256)S(1)}, f32[256]{0:T(256)}, u32[]{:S(2)}) copy-start(f32[256]{0:T(256)} %param.16) | copy-start | bytes 3076
  6.6 217.6 %copy-start.4 = (s32[256,128]{1,0:T(8,128)S(1)}, s32[256,128]{1,0:T(8,128)}, u32[]{:S(2)}) copy-start(s32[256,128]{1,0:T(8,128)} %param.15) | copy-start | bytes 393220
  6.6 98.2 %reduce-scatter.3.cloned.1.call-start = ((), (), s32[]{:S(2)}) async-start(), calls=%async_computation.2 | async-start | bytes 1392640 | tf_op jit(solution)/shard_map/reduce_scatter | solution.py:62
  24.0 142.5 %reduce-scatter.5.cloned.1.call-start = ((), (), s32[]{:S(2)}) async-start(), calls=%async_computation.3 | async-start | bytes 589824 | tf_op jit(solution)/shard_map/reduce_scatter | solution.py:117
  133.6 148.9 %all-gather.3.cloned.1.call-start = ((), (), s32[]{:S(2)}) async-start(), calls=%async_computation.4 | async-start | bytes 4456448 | tf_op jit(solution)/shard_map/all_gather | solution.py:125
  289.5 16.3 %collective-permute-start = (f32[128,512]{1,0:T(8,128)S(1)}, f32[128,512]{1,0:T(8,128)S(1)}, u32[]{:S(2)}, u32[]{:S(2)}) collective-permute-start(f32[128,512]{1,0:T(8,128)S(1)} %constant_dynamic-slice_fusion.1), channel_id=1, source_target_pairs={{0,128},{128,0},{1,129},{129,1},{2,130},{130,2},{3,131},{131,3},{4... | collective-permute-start | bytes 786440 | tf_op jit(solution)/shard_map/ppermute | solution.py:16
Sparse Core Ops, SparseCore 0:
  24.1 80.6 reduce-scatter.2
  133.7 32.7 reduce-scatter.4
  224.2 58.2 all-gather.2
where the time goes:
time: 648 us; the launch traced here: 647 us
  blocking collectives  427 us (66%)
  waiting for transfers between devices  182 us (28%)
  between operations  13.3 us (2%)
  matrix products  12.1 us (2%)
  other arithmetic  10.5 us (2%)
    psum x1, blocking collectives, body(): totals = lax.psum(jnp.sum(jnp.exp(guided), 1), ('dp', 'tensor'))  334 us
    reduce_scatter x1, waiting for transfers between devices, body(): lax.psum_scatter(jnp.concatenate([jnp.dot(all_rows, w_query, preferred_el...  79.2 us
    all_gather x1, waiting for transfers between devices, body(): lax.all_gather(normed_all, 'dp', axis=1, tiled=True)  58.3 us
    psum x1, blocking collectives, body(): squares = lax.psum(jnp.sum(widened * widened, 1), 'dp')  40.3 us
    reduce_scatter x1, waiting for transfers between devices, body(): lax.psum_scatter(partial_out, 'tensor', scatter_dimension=0, tiled=True)  32.9 us
    all_gather x1, blocking collectives, body(): lax.all_gather(attended, 'dp', axis=0, tiled=True)  23.3 us
    all_gather x1, blocking collectives, body(): normed_all = lax.all_gather(normed, 'tensor', axis=0, tiled=True)  15.3 us
    all_gather x1, blocking collectives, body(): all_rows = lax.all_gather(hidden[0], 'tensor', axis=0, tiled=True)  14.5 us
  transfers between devices with their start and end apart: 4, of which 4 were waited for; matrix products, arithmetic and copies ran while one was open for 1% of the time, Pallas kernels for 0%

commit v1 on v0

--- a/solution.py
+++ b/solution.py
@@ -8,6 +8,27 @@
 rope_theta = 500000.0
 penalty_step = 1.5
 norm_eps = 1e-05
+
+
+def collect(array, axis, dim):
+    length, index, span = (lax.axis_size(axis), lax.axis_index(axis), array.shape[dim])
+    right = [(i, (i + 1) % length) for i in range(length)]
+    downward = [(i, (i - 1) % length) for i in range(length)]
+    whole = jnp.zeros((*array.shape[:dim], length * span, *array.shape[dim + 1 :]), array.dtype)
+    whole = lax.dynamic_update_slice_in_dim(whole, array, index * span, axis=dim)
+    from_left = from_right = array
+    halfway = length // 2
+    for turn in range(1, halfway + 1):
+        from_left = lax.ppermute(from_left, axis, right)
+        whole = lax.dynamic_update_slice_in_dim(
+            whole, from_left, (index - turn) % length * span, axis=dim
+        )
+        if turn < length - halfway:
+            from_right = lax.ppermute(from_right, axis, downward)
+            whole = lax.dynamic_update_slice_in_dim(
+                whole, from_right, (index + turn) % length * span, axis=dim
+            )
+    return whole
 
 
 def partner_2(value, axis, distance):
@@ -121,11 +142,7 @@
     inverse = lax.rsqrt(squares / MODEL_WIDTH + norm_eps)
     normed = (widened * inverse[:, None] * norm_gain.astype(jnp.float32)).astype(jnp.bfloat16)
     normed_all = lax.all_gather(normed, "tensor", axis=0, tiled=True)
-    logits = jnp.dot(
-        lax.all_gather(normed_all, "dp", axis=1, tiled=True),
-        w_head,
-        preferred_element_type=jnp.float32,
-    )
+    logits = jnp.dot(collect(normed_all, "dp", 1), w_head, preferred_element_type=jnp.float32)
     stream_side = lax.axis_index("stream")
     half_rows = logits.shape[0] // 2
     mine_start = stream_side * half_rows

time: 648 us -> 671 us (1.035)
  starting transfers between devices: 0.41 us -> 42.1 us
  waiting for transfers between devices: 182 us -> 161 us
    all_gather x1 -> x0, waiting for transfers between devices: 58.3 us -> none  [body(): lax.all_gather(normed_all, 'dp', axis=1, tiled=True)]
    ppermute x0 -> x15, waiting for transfers between devices: none -> 42.3 us  [the longest x8 42 us: collect(): from_left = lax.ppermute(from_left, axis, right)]
    ppermute x0 -> x15, starting transfers between devices: none -> 39 us  [the longest x7 39 us: collect(): from_right = lax.ppermute(from_right, axis, downward)]
  transfers between devices with their start and end apart: 4 -> 18, of which waited for: 4 -> 14; matrix products, arithmetic and copies ran while one was open for 1% -> 1% of each run, Pallas kernels for 0% -> 0%
where the time goes in v1:
time: 671 us; the launch traced here: 665 us
  blocking collectives  425 us (63%)
  waiting for transfers between devices  161 us (24%)
  starting transfers between devices  42.1 us (6%)
  between operations  13.8 us (2%)
  matrix products  10.8 us (2%)
  other arithmetic  9.25 us (1%)
    psum x1, blocking collectives, body(): totals = lax.psum(jnp.sum(jnp.exp(guided), 1), ('dp', 'tensor'))  333 us
    reduce_scatter x1, waiting for transfers between devices, body(): lax.psum_scatter(jnp.concatenate([jnp.dot(all_rows, w_query, preferred_el...  80.6 us
    ppermute x8, waiting for transfers between devices, collect(): from_left = lax.ppermute(from_left, axis, right)  42 us
    psum x1, blocking collectives, body(): squares = lax.psum(jnp.sum(widened * widened, 1), 'dp')  40.3 us
    ppermute x7, starting transfers between devices, collect(): from_right = lax.ppermute(from_right, axis, downward)  39 us
    reduce_scatter x1, waiting for transfers between devices, body(): lax.psum_scatter(partial_out, 'tensor', scatter_dimension=0, tiled=True)  33 us
    all_gather x1, blocking collectives, body(): lax.all_gather(attended, 'dp', axis=0, tiled=True)  23.3 us
    all_gather x1, blocking collectives, body(): all_rows = lax.all_gather(hidden[0], 'tensor', axis=0, tiled=True)  14.5 us
  transfers between devices with their start and end apart: 18, of which 14 were waited for; matrix products, arithmetic and copies ran while one was open for 1% of the time, Pallas kernels for 0%

profile of v1, /device:TPU:128, one launch (start us, length us, event | category | flops | bytes accessed | tf_op | source)
XLA Modules:
  0.0 665.3 jit_solution(11992731392597239653)
XLA Ops:
  6.5 14.5 %all-gather = bf16[1,256,512]{2,1,0:T(8,128)(2,1)S(1)} all-gather(bf16[1,32,512]{2,1,0:T(8,128)(2,1)} %param.11), channel_id=2, replica_groups=mesh['stream'=2,'dp'=16,'tensor'=8] {'tensor'}, dimensions={1}, use_global_device_ids=true | all-gather | bytes 294912 | tf_op jit(solution)/shard_map/all_gather | solution.py:81
  21.1 0.4 fusion.9
  21.5 1.2 fusion.5
  22.7 1.2 pad_maximum_fusion
  24.0 0.1 iota_compare_fusion
  24.1 0.1 multiply_cosine_fusion.1
  24.2 80.6 %reduce-scatter.3.cloned.1.call-done = f32[16,1280]{1,0:T(8,128)} async-done(((f32[256,1280]{1,0:T(8,128)}), f32[16,1280]{1,0:T(8,128)}) %reduce-scatter.3.cloned.1.call-update) | async-done | bytes 81936 | tf_op jit(solution)/shard_map/reduce_scatter | solution.py:83
  104.9 0.7 slice.36
  105.6 0.1 fusion.30
  105.7 0.8 slice_bitcast_fusion
  106.6 0.1 maximum_bitcast_fusion
  106.7 0.1 subtract_convert_fusion
  106.8 0.2 fusion.25
  107.0 0.5 fusion.33
  107.5 0.3 fusion.2
  107.9 23.3 %all_gather.10 = bf16[256,1024]{1,0:T(8,128)(2,1)S(1)} all-gather(bf16[16,1024]{1,0:T(8,128)(2,1)S(1)} %bitcast.51), channel_id=1, replica_groups=mesh['stream'=2,'dp'=16,'tensor'=8] {'dp'}, dimensions={0}, use_global_device_ids=true | all-gather | bytes 557056 | tf_op jit(solution)/shard_map/all_gather | solution.py:134
  131.1 2.5 fusion.34
  133.7 33.0 %reduce-scatter.5.cloned.1.call-done = f32[32,512]{1,0:T(8,128)} async-done(((f32[256,512]{1,0:T(8,128)}), f32[32,512]{1,0:T(8,128)}) %reduce-scatter.5.cloned.1.call-update) | async-done | bytes 65552 | tf_op jit(solution)/shard_map/reduce_scatter | solution.py:138
  166.6 1.0 fusion.11
  167.6 40.3 %psum.14 = f32[32]{0:T(128)S(1)} all-reduce(f32[32]{0:T(128)S(1)} %fusion.11), channel_id=1, replica_groups=mesh['stream'=2,'dp'=16,'tensor'=8] {'dp'}, use_global_device_ids=true, to_apply=%region_4.5 | all-reduce | flops 32 | bytes 256 | tf_op jit(solution)/shard_map/psum | solution.py:141
  207.9 0.9 fusion.13
  208.8 14.2 %all_gather.11 = bf16[256,512]{1,0:T(8,128)(2,1)S(1)} all-gather(bf16[32,512]{1,0:T(8,128)(2,1)S(1)} %fusion.13), channel_id=1, replica_groups=mesh['stream'=2,'dp'=16,'tensor'=8] {'tensor'}, dimensions={0}, use_global_device_ids=true | all-gather | bytes 294912 | tf_op jit(solution)/shard_map/all_gather | solution.py:144
  223.0 5.3 collective-permute-start.1
  228.3 6.5 collective-permute-done
  234.9 5.3 collective-permute-start.3
  240.2 5.7 collective-permute-done.2
  245.9 5.4 collective-permute-start.5
  251.4 4.6 collective-permute-done.4
  256.0 0.5 broadcast_in_dim.10
  256.6 5.4 collective-permute-start.7
  262.0 3.7 collective-permute-done.6
  265.8 0.1 collective-permute-done.7
  265.9 5.8 collective-permute-start.9
  271.7 3.7 collective-permute-done.8
  275.5 0.1 collective-permute-done.9
  275.6 5.8 collective-permute-start.11
  281.4 3.7 collective-permute-done.10
  285.2 0.1 collective-permute-done.11
  285.3 5.8 collective-permute-start.13
  291.2 4.6 collective-permute-done.12
  295.8 9.6 %collective-permute-done.14 = bf16[256,512]{1,0:T(8,128)(2,1)S(1)} collective-permute-done((bf16[256,512]{1,0:T(8,128)(2,1)S(1)}, bf16[256,512]{1,0:T(8,128)(2,1)S(1)}, u32[]{:S(2)}, u32[]{:S(2)}) %collective-permute-start.14) | collective-permute-done | bytes 262176 | tf_op jit(solution)/shard_map/ppermute | solution.py:22
  305.4 5.7 fusion.35
  311.2 3.0 collective-permute-start.15
  314.2 4.6 convert_reduce_fusion
  318.9 5.5 collective-permute-done.15
  324.4 0.2 exponential_reduce_fusion
  324.6 333.1 %psum.15 = f32[128]{0:T(128)S(1)} all-reduce(f32[128]{0:T(128)S(1)} %get-tuple-element.5), channel_id=1, replica_groups=mesh['stream'=2,'dp'=16,'tensor'=8] {'dp','tensor'}, use_global_device_ids=true, to_apply=%region_7.8 | all-reduce | flops 128 | bytes 1024 | tf_op jit(solution)/shard_map/psum | solution.py:160
  657.7 0.8 broadcast_subtract_fusion
  (63 shorter events, 0.8 us)
Async XLA Ops:
  6.5 14.5 %copy-start = (bf16[512,1024]{1,0:T(8,128)(2,1)S(1)}, bf16[512,1024]{1,0:T(8,128)(2,1)}, u32[]{:S(2)}) copy-start(bf16[512,1024]{1,0:T(8,128)(2,1)} %param.17) | copy-start | bytes 3145732
  6.5 17.5 %copy-start.6 = (s32[1,16]{1,0:T(1,128)S(1)}, s32[1,16]{1,0:T(1,128)}, u32[]{:S(2)}) copy-start(s32[1,16]{1,0:T(1,128)} %param.14) | copy-start | bytes 196
  6.5 100.5 %copy-start.1 = (bf16[1,16,1,256,128]{4,3,2,1,0:T(8,128)(2,1)S(1)}, bf16[1,16,1,256,128]{4,3,2,1,0:T(8,128)(2,1)}, u32[]{:S(2)}) copy-start(bf16[1,16,1,256,128]{4,3,2,1,0:T(8,128)(2,1)} %param.12) | copy-start | bytes 3145732
  6.5 98.3 %reduce-scatter.3.cloned.1.call-start = ((), (), s32[]{:S(2)}) async-start(), calls=%async_computation.2 | async-start | bytes 1392640 | tf_op jit(solution)/shard_map/reduce_scatter | solution.py:83
  21.1 86.5 %copy-start.2 = (bf16[1,16,1,256,128]{4,3,2,1,0:T(8,128)(2,1)S(1)}, bf16[1,16,1,256,128]{4,3,2,1,0:T(8,128)(2,1)}, u32[]{:S(2)}) copy-start(bf16[1,16,1,256,128]{4,3,2,1,0:T(8,128)(2,1)} %param.13) | copy-start | bytes 3145732
  23.9 109.7 %copy-start.5 = (bf16[512]{0:T(512)(128)(2,1)S(1)}, bf16[512]{0:T(512)(128)(2,1)}, u32[]{:S(2)}) copy-start(bf16[512]{0:T(512)(128)(2,1)} %param.20) | copy-start | bytes 3076
  23.9 142.7 %copy-start.3 = (bf16[1,32,512]{2,1,0:T(8,128)(2,1)S(1)}, bf16[1,32,512]{2,1,0:T(8,128)(2,1)}, u32[]{:S(2)}) copy-start(bf16[1,32,512]{2,1,0:T(8,128)(2,1)} %param.11) | copy-start | bytes 98308
  23.9 222.0 %copy-start.4 = (s32[256,128]{1,0:T(8,128)S(1)}, s32[256,128]{1,0:T(8,128)}, u32[]{:S(2)}) copy-start(s32[256,128]{1,0:T(8,128)} %param.15) | copy-start | bytes 393220
  23.9 227.4 %copy-start.7 = (f32[256]{0:T(256)S(1)}, f32[256]{0:T(256)}, u32[]{:S(2)}) copy-start(f32[256]{0:T(256)} %param.16) | copy-start | bytes 3076
  23.9 142.7 %reduce-scatter.5.cloned.1.call-start = ((), (), s32[]{:S(2)}) async-start(), calls=%async_computation.3 | async-start | bytes 589824 | tf_op jit(solution)/shard_map/reduce_scatter | solution.py:138
  223.0 11.9 %collective-permute-start = (bf16[256,512]{1,0:T(8,128)(2,1)S(1)}, bf16[256,512]{1,0:T(8,128)(2,1)S(1)}, u32[]{:S(2)}, u32[]{:S(2)}) collective-permute-start(bf16[256,512]{1,0:T(8,128)(2,1)S(1)} %all_gather.11), channel_id=1, source_target_pairs={{0,8},{8,16},{16,24},{24,32},{32,40},{40,48},{48,56},{56,64},{64,7... | collective-permute-start | bytes 786440 | tf_op jit(solution)/shard_map/ppermute | solution.py:22
  223.0 11.9 %collective-permute-start.1 = (bf16[256,512]{1,0:T(8,128)(2,1)S(1)}, bf16[256,512]{1,0:T(8,128)(2,1)S(1)}, u32[]{:S(2)}, u32[]{:S(2)}) collective-permute-start(bf16[256,512]{1,0:T(8,128)(2,1)S(1)} %all_gather.11), channel_id=1, source_target_pairs={{0,120},{8,0},{16,8},{24,16},{32,24},{40,32},{48,40},{56,48},{64,5... | collective-permute-start | bytes 786440 | tf_op jit(solution)/shard_map/ppermute | solution.py:27
  234.9 11.0 %collective-permute-start.2 = (bf16[256,512]{1,0:T(8,128)(2,1)S(1)}, bf16[256,512]{1,0:T(8,128)(2,1)S(1)}, u32[]{:S(2)}, u32[]{:S(2)}) collective-permute-start(bf16[256,512]{1,0:T(8,128)(2,1)S(1)} %collective-permute-done), channel_id=1, source_target_pairs={{0,8},{8,16},{16,24},{24,32},{32,40},{40,48},{48,56},{56,64},{64,7... | collective-permute-start | bytes 786440 | tf_op jit(solution)/shard_map/ppermute | solution.py:22
  234.9 11.0 %collective-permute-start.3 = (bf16[256,512]{1,0:T(8,128)(2,1)S(1)}, bf16[256,512]{1,0:T(8,128)(2,1)S(1)}, u32[]{:S(2)}, u32[]{:S(2)}) collective-permute-start(bf16[256,512]{1,0:T(8,128)(2,1)S(1)} %collective-permute-done.1), channel_id=1, source_target_pairs={{0,120},{8,0},{16,8},{24,16},{32,24},{40,32},{48,40},{56,48},{64,5... | collective-permute-start | bytes 786440 | tf_op jit(solution)/shard_map/ppermute | solution.py:27
  245.9 10.2 %collective-permute-start.4 = (bf16[256,512]{1,0:T(8,128)(2,1)S(1)}, bf16[256,512]{1,0:T(8,128)(2,1)S(1)}, u32[]{:S(2)}, u32[]{:S(2)}) collective-permute-start(bf16[256,512]{1,0:T(8,128)(2,1)S(1)} %collective-permute-done.2), channel_id=1, source_target_pairs={{0,8},{8,16},{16,24},{24,32},{32,40},{40,48},{48,56},{56,64},{64,7... | collective-permute-start | bytes 786440 | tf_op jit(solution)/shard_map/ppermute | solution.py:22
  245.9 10.7 %collective-permute-start.5 = (bf16[256,512]{1,0:T(8,128)(2,1)S(1)}, bf16[256,512]{1,0:T(8,128)(2,1)S(1)}, u32[]{:S(2)}, u32[]{:S(2)}) collective-permute-start(bf16[256,512]{1,0:T(8,128)(2,1)S(1)} %collective-permute-done.3), channel_id=1, source_target_pairs={{0,120},{8,0},{16,8},{24,16},{32,24},{40,32},{48,40},{56,48},{64,5... | collective-permute-start | bytes 786440 | tf_op jit(solution)/shard_map/ppermute | solution.py:27
  256.0 9.7 %collective-permute-start.6 = (bf16[256,512]{1,0:T(8,128)(2,1)S(1)}, bf16[256,512]{1,0:T(8,128)(2,1)S(1)}, u32[]{:S(2)}, u32[]{:S(2)}) collective-permute-start(bf16[256,512]{1,0:T(8,128)(2,1)S(1)} %collective-permute-done.4), channel_id=1, source_target_pairs={{0,8},{8,16},{16,24},{24,32},{32,40},{40,48},{48,56},{56,64},{64,7... | collective-permute-start | bytes 786440 | tf_op jit(solution)/shard_map/ppermute | solution.py:22
  256.6 9.3 %collective-permute-start.7 = (bf16[256,512]{1,0:T(8,128)(2,1)S(1)}, bf16[256,512]{1,0:T(8,128)(2,1)S(1)}, u32[]{:S(2)}, u32[]{:S(2)}) collective-permute-start(bf16[256,512]{1,0:T(8,128)(2,1)S(1)} %collective-permute-done.5), channel_id=1, source_target_pairs={{0,120},{8,0},{16,8},{24,16},{32,24},{40,32},{48,40},{56,48},{64,5... | collective-permute-start | bytes 786440 | tf_op jit(solution)/shard_map/ppermute | solution.py:27
  265.7 9.7 %collective-permute-start.8 = (bf16[256,512]{1,0:T(8,128)(2,1)S(1)}, bf16[256,512]{1,0:T(8,128)(2,1)S(1)}, u32[]{:S(2)}, u32[]{:S(2)}) collective-permute-start(bf16[256,512]{1,0:T(8,128)(2,1)S(1)} %collective-permute-done.6), channel_id=1, source_target_pairs={{0,8},{8,16},{16,24},{24,32},{32,40},{40,48},{48,56},{56,64},{64,7... | collective-permute-start | bytes 786440 | tf_op jit(solution)/shard_map/ppermute | solution.py:22
  265.9 9.7 %collective-permute-start.9 = (bf16[256,512]{1,0:T(8,128)(2,1)S(1)}, bf16[256,512]{1,0:T(8,128)(2,1)S(1)}, u32[]{:S(2)}, u32[]{:S(2)}) collective-permute-start(bf16[256,512]{1,0:T(8,128)(2,1)S(1)} %collective-permute-done.7), channel_id=1, source_target_pairs={{0,120},{8,0},{16,8},{24,16},{32,24},{40,32},{48,40},{56,48},{64,5... | collective-permute-start | bytes 786440 | tf_op jit(solution)/shard_map/ppermute | solution.py:27
  275.4 9.7 %collective-permute-start.10 = (bf16[256,512]{1,0:T(8,128)(2,1)S(1)}, bf16[256,512]{1,0:T(8,128)(2,1)S(1)}, u32[]{:S(2)}, u32[]{:S(2)}) collective-permute-start(bf16[256,512]{1,0:T(8,128)(2,1)S(1)} %collective-permute-done.8), channel_id=1, source_target_pairs={{0,8},{8,16},{16,24},{24,32},{32,40},{40,48},{48,56},{56,64},{64,7... | collective-permute-start | bytes 786440 | tf_op jit(solution)/shard_map/ppermute | solution.py:22
  275.6 9.7 %collective-permute-start.11 = (bf16[256,512]{1,0:T(8,128)(2,1)S(1)}, bf16[256,512]{1,0:T(8,128)(2,1)S(1)}, u32[]{:S(2)}, u32[]{:S(2)}) collective-permute-start(bf16[256,512]{1,0:T(8,128)(2,1)S(1)} %collective-permute-done.9), channel_id=1, source_target_pairs={{0,120},{8,0},{16,8},{24,16},{32,24},{40,32},{48,40},{56,48},{64,5... | collective-permute-start | bytes 786440 | tf_op jit(solution)/shard_map/ppermute | solution.py:27
  285.1 10.6 %collective-permute-start.12 = (bf16[256,512]{1,0:T(8,128)(2,1)S(1)}, bf16[256,512]{1,0:T(8,128)(2,1)S(1)}, u32[]{:S(2)}, u32[]{:S(2)}) collective-permute-start(bf16[256,512]{1,0:T(8,128)(2,1)S(1)} %collective-permute-done.10), channel_id=1, source_target_pairs={{0,8},{8,16},{16,24},{24,32},{32,40},{40,48},{48,56},{56,64},{64,7... | collective-permute-start | bytes 786440 | tf_op jit(solution)/shard_map/ppermute | solution.py:22
  285.3 10.5 %collective-permute-start.13 = (bf16[256,512]{1,0:T(8,128)(2,1)S(1)}, bf16[256,512]{1,0:T(8,128)(2,1)S(1)}, u32[]{:S(2)}, u32[]{:S(2)}) collective-permute-start(bf16[256,512]{1,0:T(8,128)(2,1)S(1)} %collective-permute-done.11), channel_id=1, source_target_pairs={{0,120},{8,0},{16,8},{24,16},{32,24},{40,32},{48,40},{56,48},{64,5... | collective-permute-start | bytes 786440 | tf_op jit(solution)/shard_map/ppermute | solution.py:27
  295.7 9.7 %collective-permute-start.14 = (bf16[256,512]{1,0:T(8,128)(2,1)S(1)}, bf16[256,512]{1,0:T(8,128)(2,1)S(1)}, u32[]{:S(2)}, u32[]{:S(2)}) collective-permute-start(bf16[256,512]{1,0:T(8,128)(2,1)S(1)} %collective-permute-done.12), channel_id=1, source_target_pairs={{0,8},{8,16},{16,24},{24,32},{32,40},{40,48},{48,56},{56,64},{64,7... | collective-permute-start | bytes 786440 | tf_op jit(solution)/shard_map/ppermute | solution.py:22
  311.2 13.2 %collective-permute-start.15 = (f32[128,512]{1,0:T(8,128)S(1)}, f32[128,512]{1,0:T(8,128)S(1)}, u32[]{:S(2)}, u32[]{:S(2)}) collective-permute-start(f32[128,512]{1,0:T(8,128)S(1)} %constant_dynamic-slice_fusion.1), channel_id=1, source_target_pairs={{0,128},{128,0},{1,129},{129,1},{2,130},{130,2},{3,131},{131,3},{4... | collective-permute-start | bytes 786440 | tf_op jit(solution)/shard_map/ppermute | solution.py:37
Sparse Core Ops, SparseCore 0:
  24.1 80.7 reduce-scatter.2
  133.8 32.8 reduce-scatter.4
